TPU v7x, 128 devices: a whole 4x4x4 slice. The times are simulated.
128 devices in a mesh: fsdp: 2 (over core), ctx: 64 (over z, x, y).
Axes of the slice: x: 4, y: 4, z: 4, core: 2. Of those that a mesh axis runs over, the one named last changes fastest.
Arguments:
- token_ids: int32 [2, 8192], P('fsdp', 'ctx'), may hold values from 0 to 511
- embedding: bfloat16 [512, 4096], P(None, 'fsdp'), may hold values from -5 to 5
- conv_taps: float32 [3, 3, 4096], replicated, may hold values from -2.5 to 2.5
- residues: float32 [4096, 16], replicated, may hold values from -1.2 to 1.2
- decays: float32 [4096, 16], replicated, may hold values from 2.4414062e-06 to 0.05
- filter_seed: int32 [4096, 16], replicated, may hold values from 0 to 4095
- skip_gain: float32 [4096], replicated, may hold values from 0.5 to 1.5
- cotangent: float32 [2, 4096, 8192], P('fsdp', None, 'ctx'), may hold values from -6 to 6
Outputs:
- mixer_out: float32 [2, 4096, 8192], P('fsdp', None, 'ctx')
- embed_grad: float32 [512, 4096], P(None, 'fsdp')
All inputs are finite; a program needn't handle non-finite values.
Results may differ from a plain program's by a relative error of at most 0.0006.
Values may be sent and summed in bfloat16 or wider, within the bound.
A program may use at most 320 MiB of HBM per device.

v0:
```python
import math
import jax
import jax.numpy as jnp
from jax import lax
from jax.sharding import PartitionSpec as P

PERIOD = 4096
HIGHEST = lax.Precision.HIGHEST
TWO_PI = 2.0 * math.pi


def from_behind(value, axis, steps):
    count = lax.axis_size(axis)
    leading, last = (max(0, -steps), min(count, count - steps))
    return lax.ppermute(value, axis, [(source, source + steps) for source in range(leading, last)])


def dft_tables(half_blocks, tok_block):
    full_blocks = 2 * half_blocks
    total_len = full_blocks * tok_block
    outer = (
        jnp.arange(half_blocks, dtype=jnp.int32)[:, None]
        * jnp.arange(full_blocks, dtype=jnp.int32)[None, :]
        % full_blocks
    )
    outer_angle = TWO_PI / full_blocks * outer.astype(jnp.float32)
    twist = (
        jnp.arange(full_blocks, dtype=jnp.int32)[:, None]
        * jnp.arange(tok_block, dtype=jnp.int32)[None, :]
        % total_len
    )
    twist_angle = TWO_PI / total_len * twist.astype(jnp.float32)
    inner = (
        jnp.arange(tok_block, dtype=jnp.int32)[:, None]
        * jnp.arange(tok_block, dtype=jnp.int32)[None, :]
        % tok_block
    )
    inner_angle = TWO_PI / tok_block * inner.astype(jnp.float32)
    return (
        jnp.cos(outer_angle),
        jnp.sin(outer_angle),
        jnp.cos(twist_angle),
        jnp.sin(twist_angle),
        jnp.cos(inner_angle),
        jnp.sin(inner_angle),
    )


def forward_dft(blocks, tables):
    outer_cos, outer_sin, twist_cos, twist_sin, inner_cos, inner_sin = tables
    part_real = jnp.einsum("bcst,sk->bckt", blocks, outer_cos, precision=HIGHEST)
    part_imag = -jnp.einsum("bcst,sk->bckt", blocks, outer_sin, precision=HIGHEST)
    turned_real = part_real * twist_cos + part_imag * twist_sin
    turned_imag = part_imag * twist_cos - part_real * twist_sin
    spec_real = jnp.einsum("bckt,tm->bckm", turned_real, inner_cos, precision=HIGHEST) + jnp.einsum(
        "bckt,tm->bckm", turned_imag, inner_sin, precision=HIGHEST
    )
    spec_imag = jnp.einsum("bckt,tm->bckm", turned_imag, inner_cos, precision=HIGHEST) - jnp.einsum(
        "bckt,tm->bckm", turned_real, inner_sin, precision=HIGHEST
    )
    return (spec_real, spec_imag)


def inverse_dft(prod_real, prod_imag, tables):
    outer_cos, outer_sin, twist_cos, twist_sin, inner_cos, inner_sin = tables
    total_len = outer_cos.shape[1] * inner_cos.shape[0]
    back_real = jnp.einsum("bckm,tm->bckt", prod_real, inner_cos, precision=HIGHEST) - jnp.einsum(
        "bckm,tm->bckt", prod_imag, inner_sin, precision=HIGHEST
    )
    back_imag = jnp.einsum("bckm,tm->bckt", prod_imag, inner_cos, precision=HIGHEST) + jnp.einsum(
        "bckm,tm->bckt", prod_real, inner_sin, precision=HIGHEST
    )
    turned_real = back_real * twist_cos - back_imag * twist_sin
    turned_imag = back_imag * twist_cos + back_real * twist_sin
    signal = jnp.einsum("bckt,sk->bcst", turned_real, outer_cos, precision=HIGHEST) - jnp.einsum(
        "bckt,sk->bcst", turned_imag, outer_sin, precision=HIGHEST
    )
    return signal / total_len


def apply_filter(spread, kernel_real, kernel_imag, tables, adjoint_sign):
    batch_rows = spread.shape[0]
    slab_size = spread.shape[1]
    half_blocks = tables[0].shape[0]
    tok_block = tables[4].shape[0]
    spec_real, spec_imag = forward_dft(
        spread.reshape(batch_rows, slab_size, half_blocks, tok_block), tables
    )
    prod_real = kernel_real * spec_real - adjoint_sign * kernel_imag * spec_imag
    prod_imag = kernel_real * spec_imag + adjoint_sign * kernel_imag * spec_real
    return inverse_dft(prod_real, prod_imag, tables).reshape(spread.shape)


def body(token_ids, embedding, conv_taps, residues, decays, filter_seed, skip_gain, cotangent):
    ctx_size = lax.axis_size("ctx")
    ctx_rank = lax.axis_index("ctx")
    model_width = conv_taps.shape[2]
    vocab_size = embedding.shape[0]
    tok_block = token_ids.shape[1]
    full_table = lax.all_gather(embedding, "fsdp", axis=1, tiled=True)
    gain_local = skip_gain[:, None]
    signal = jnp.swapaxes(jnp.take(full_table, token_ids, axis=0), 1, 2)
    before = from_behind(signal[:, :, tok_block - 2 :], "ctx", 1)
    extended = jnp.concatenate([before, signal], axis=2).astype(jnp.float32)

    def causal_mix(tap_set):
        return (
            tap_set[0][:, None] * extended[:, :, 2:]
            + tap_set[1][:, None] * extended[:, :, 1 : tok_block + 1]
            + tap_set[2][:, None] * extended[:, :, :tok_block]
        )

    query_stream = causal_mix(conv_taps[0])
    key_stream = causal_mix(conv_taps[1])
    value_stream = causal_mix(conv_taps[2])
    mixed_in = key_stream * value_stream
    grad_long = cotangent * query_stream
    seq_len = tok_block * ctx_size
    slab_size = model_width // ctx_size
    slab_start = ctx_rank * slab_size
    positions = jnp.arange(seq_len, dtype=jnp.int32)
    decay_rate = lax.dynamic_slice_in_dim(decays, slab_start, slab_size, 0)[:, :, None]
    seed_part = lax.dynamic_slice_in_dim(filter_seed, slab_start, slab_size, 0)[:, :, None]
    residue_part = lax.dynamic_slice_in_dim(residues, slab_start, slab_size, 0)[:, :, None]
    phase_int = seed_part * positions[None, None, :] % PERIOD
    weight = residue_part * jnp.sqrt(decay_rate + 1.0 / seq_len)
    kernel = jnp.sum(
        weight
        * jnp.exp(-decay_rate * positions.astype(jnp.float32)[None, None, :])
        * jnp.cos(TWO_PI / PERIOD * phase_int.astype(jnp.float32)),
        axis=1,
    )
    tables = dft_tables(ctx_size, tok_block)
    kernel_real, kernel_imag = forward_dft(
        kernel.reshape(1, slab_size, ctx_size, tok_block), tables
    )
    spread_mix, spread_grad = (
        lax.all_to_all(mixed_in, "ctx", split_axis=1, concat_axis=2, tiled=True),
        lax.all_to_all(grad_long, "ctx", split_axis=1, concat_axis=2, tiled=True),
    )
    conv_part = apply_filter(spread_mix, kernel_real, kernel_imag, tables, 1.0)
    corr_part = apply_filter(spread_grad, kernel_real, kernel_imag, tables, -1.0)
    conv_out, correlated = (
        lax.all_to_all(conv_part, "ctx", split_axis=2, concat_axis=1, tiled=True),
        lax.all_to_all(corr_part, "ctx", split_axis=2, concat_axis=1, tiled=True),
    )
    long_out = conv_out + gain_local * mixed_in
    mixer_local = query_stream * long_out
    grad_query = cotangent * long_out
    grad_mixed = correlated + gain_local * grad_long
    grad_key = grad_mixed * value_stream
    grad_value = grad_mixed * key_stream

    def tap_term(tap_index):
        return (
            conv_taps[0][tap_index][:, None] * grad_query
            + conv_taps[1][tap_index][:, None] * grad_key
            + conv_taps[2][tap_index][:, None] * grad_value
        )

    first_term = tap_term(0)
    second_term = tap_term(1)
    third_term = tap_term(2)
    next_rows = from_behind(jnp.stack([second_term[:, :, :2], third_term[:, :, :2]]), "ctx", -1)
    grad_signal = (
        first_term
        + jnp.concatenate([second_term, next_rows[0]], axis=2)[:, :, 1 : tok_block + 1]
        + jnp.concatenate([third_term, next_rows[1]], axis=2)[:, :, 2 : tok_block + 2]
    )
    one_hot = (
        token_ids[:, :, None] == jnp.arange(vocab_size, dtype=jnp.int32)[None, None, :]
    ).astype(jnp.float32)
    partial_grad = jnp.einsum("btv,bct->vc", one_hot, grad_signal, precision=HIGHEST)
    half_grad = lax.psum_scatter(partial_grad, "fsdp", scatter_dimension=1, tiled=True)
    embed_grad = lax.psum(half_grad, "ctx")
    return (mixer_local, embed_grad)


def solution(mesh):
    placed = (P("fsdp", "ctx"), P(None, "fsdp"), P(), P(), P(), P(), P(), P("fsdp", None, "ctx"))
    return jax.shard_map(
        body,
        mesh=mesh,
        in_specs=placed,
        out_specs=(P("fsdp", None, "ctx"), P(None, "fsdp")),
        check_vma=False,
    )
```

profile of v0, /device:TPU:0, one launch (start us, length us, event | category | flops | bytes accessed | tf_op | source)
XLA Modules:
  0.0 764.9 jit_solution(1966881312093857230)
XLA Ops:
  12.0 16.5 %all-gather.2.cloned.1.call-done = bf16[512,4096]{1,0:T(8,128)(2,1)} async-done(((bf16[512,2048]{1,0:T(8,128)(2,1)}), bf16[512,4096]{1,0:T(8,128)(2,1)}) %all-gather.2.cloned.1.call-update) | async-done | bytes 4194320 | tf_op jit(solution)/shard_map/all_gather | solution.py:100
  52.2 10.4 %all-to-all-start.2 = ((f32[1,4096,128]{2,0,1:T(1,128)}), f32[1,4096,128]{2,0,1:T(1,128)S(1)}, u32[]{:S(2)}, u32[]{:S(2)}) async-start(f32[1,4096,128]{2,0,1:T(1,128)} %copy.93), calls=%async_computation.2 | async-start | bytes 4194304 | tf_op jit(solution)/shard_map/all_to_all | solution.py:139
  62.6 133.4 %fusion.5 = f32[64,8192]{1,0:T(8,128)S(1)} fusion(s32[64,16]{1,0:T(8,128)S(1)} %copy.84, f32[8192]{0:T(1024)S(1)} %copy-done.32, f32[64,16]{1,0:T(8,128)S(1)} %copy.83, f32[64,16]{1,0:T(8,128)S(1)} %copy.82), kind=kLoop, calls=%fused_computation.9 | loop fusion | flops 150470656 | bytes 2142208 | tf_op jit(solution)/shard_map/reduce_sum | solution.py:127
  204.2 5.8 fusion.27
  221.2 10.9 %all-to-all-start = ((f32[1,4096,128]{2,0,1:T(1,128)}), f32[1,4096,128]{2,0,1:T(1,128)}, u32[]{:S(2)}, u32[]{:S(2)}) async-start(f32[1,4096,128]{2,0,1:T(1,128)} %copy.85), calls=%async_computation | async-start | bytes 4194304 | tf_op jit(solution)/shard_map/all_to_all | solution.py:138
  232.2 8.8 %fusion.58 = f32[64,128,128]{2,1,0:T(8,128)} fusion(f32[64,128,128]{2,1,0:T(8,128)} %fusion.27, f32[128,64,128]{2,0,1:T(8,128)} %copy-done.6, f32[128,64,128]{2,0,1:T(8,128)} %copy-done.4, f32[128,128]{1,0:T(8,128)S(1)} %get-tuple-element.45, f32[128,128]{1,0:T(8,128)S(1)} %get-tuple-element.46), kind=kOutput, calls=%fused_computation.76 | convolution fusion | flops 1616084992 | bytes 16908288 | tf_op jit(solution)/shard_map/bckt,tm->bckm/dot_general | solution.py:58
  242.0 5.7 fusion.55
  247.7 7.0 fusion.81
  254.7 7.3 fusion.83
  262.1 6.3 fusion.85
  268.4 6.3 fusion.87
  287.4 5.7 fusion.11
  293.1 6.0 fusion.64
  299.1 5.8 fusion.61
  304.9 5.8 fusion.70
  310.8 19.4 %multiply_add_fusion = (f32[64,128,128]{2,1,0:T(8,128)}, f32[64,128,128]{2,1,0:T(8,128)}, f32[64,128,128]{2,1,0:T(8,128)}, f32[64,128,128]{2,1,0:T(8,128)}) fusion(f32[64,128,128]{2,1,0:T(8,128)} %fusion.55, f32[64,128,128]{2,1,0:T(8,128)} %fusion.70, f32[64,128,128]{2,1,0:T(8,128)} %fusion.58, f32[64,128,128]{2,1,0:T(8,128)} %fusion.64, ...), kind=kOutput, calls=%fused_computation.63 | convolution fusion | flops 1629716480 | bytes 50462720 | tf_op jit(solution)/shard_map/bckt,tm->bckm/dot_general | solution.py:55
  330.1 6.5 fusion.147
  357.7 38.4 %reduce.2 = f32[8192,64]{1,0:T(8,128)} reduce(f32[8192,1,64]{2,1,0:T(1,128)} %bitcast.330, f32[]{:T(128)} %broadcast.309), dimensions={1}, to_apply=%bitcast.304.reduce_sub_computation | reduce | bytes 4194308
  401.6 10.7 %all-to-all-start.3 = ((f32[64,1,8192]{2,1,0:T(1,128)}), f32[64,1,8192]{2,1,0:T(1,128)}, u32[]{:S(2)}, u32[]{:S(2)}) async-start(f32[64,1,8192]{2,1,0:T(1,128)} %reshape.405), calls=%async_computation.3 | async-start | bytes 4194304 | tf_op jit(solution)/shard_map/all_to_all | solution.py:145
  412.3 6.4 fusion.155
  439.2 38.4 %reduce = f32[8192,64]{1,0:T(8,128)} reduce(f32[8192,1,64]{2,1,0:T(1,128)} %bitcast.331, f32[]{:T(128)} %broadcast.309), dimensions={1}, to_apply=%bitcast.302.reduce_sub_computation | reduce | bytes 4194308
  483.1 10.5 %all-to-all-start.1 = ((f32[64,1,8192]{2,1,0:T(1,128)}), f32[64,1,8192]{2,1,0:T(1,128)}, u32[]{:S(2)}, u32[]{:S(2)}) async-start(f32[64,1,8192]{2,1,0:T(1,128)} %reshape.403), calls=%async_computation.1 | async-start | bytes 4194304 | tf_op jit(solution)/shard_map/all_to_all | solution.py:144
  494.0 7.5 reduce.3
  501.6 6.6 reshape.406
  508.1 9.1 %copy.96 = f32[1,64,8192]{2,0,1:T(1,128)S(1)} copy(f32[1,64,8192]{1,0,2:T(1,128)} %bitcast.328) | data formatting | bytes 4194304 | tf_op jit(solution)/shard_map/all_to_all | solution.py:145
  522.7 7.5 reduce.1
  530.2 6.8 reshape.404
  536.9 10.5 %copy.88 = f32[1,64,8192]{2,0,1:T(1,128)} copy(f32[1,64,8192]{1,0,2:T(1,128)} %bitcast.329) | data formatting | bytes 4194304 | tf_op jit(solution)/shard_map/all_to_all | solution.py:144
  554.7 10.9 %multiply_add_fusion.3 = (f32[1,4096,128]{1,2,0:T(8,128)}, f32[1,4096,128]{1,2,0:T(8,128)}, f32[1,4096,128]{1,2,0:T(8,128)}, f32[1,4096,128]{1,2,0:T(8,128)}, f32[1,4096,128]{1,2,0:T(8,128)}) fusion(f32[4096]{0:T(1024)S(1)} %bitcast.354, f32[4096]{0:T(1024)S(1)} %bitcast.350, f32[4096]{0:T(1024)S(1)} %bitcast.352, f32[1,4096,128]{1,2,0:T(8,128)S(1)} %copy-done.13, ...), kind=kLoop, calls=%fused_computation.102 | loop fusion | flops 6815744 | bytes 27328512 | tf_op jit(solution)/shard_map/add | solution.py:156
  576.5 6.5 fusion.75
  583.0 24.6 %reduce-scatter.2.cloned.1.call-done = f32[512,2048]{1,0:T(8,128)} async-done(((f32[512,4096]{1,0:T(8,128)}), f32[512,2048]{1,0:T(8,128)}) %reduce-scatter.2.cloned.1.call-update) | async-done | bytes 4194320 | tf_op jit(solution)/shard_map/reduce_scatter | solution.py:174
  609.5 144.1 %all-reduce.2.cloned.1.call-done = f32[512,2048]{1,0:T(8,128)} async-done(((f32[512,2048]{1,0:T(8,128)}), f32[512,2048]{1,0:T(8,128)}) %all-reduce.2.cloned.1.call-update) | async-done | bytes 4194320 | tf_op jit(solution)/shard_map/psum | solution.py:175
  (136 shorter events, 144.2 us)
Async XLA Ops:
  7.2 31.2 %copy-start = (s32[4096,16]{0,1:T(8,128)S(1)}, s32[4096,16]{0,1:T(8,128)}, u32[]{:S(2)}) copy-start(s32[4096,16]{0,1:T(8,128)} %param.13) | copy-start | bytes 786436
  7.2 21.3 %all-gather.2.cloned.1.call-start = ((), (), s32[]{:S(2)}) async-start(), calls=%async_computation.5 | async-start | bytes 6291456 | tf_op jit(solution)/shard_map/all_gather | solution.py:100
  11.9 29.8 %copy-start.20 = (f32[1,1,4096]{2,1,0:T(1,128)}, f32[1,1,4096]{2,1,0:T(1,128)S(1)}, u32[]{:S(2)}) copy-start(f32[1,1,4096]{2,1,0:T(1,128)S(1)} %get-tuple-element.36) | copy-start | bytes 49156
  11.9 29.8 %copy-start.22 = (f32[1,1,4096]{2,1,0:T(1,128)}, f32[1,1,4096]{2,1,0:T(1,128)S(1)}, u32[]{:S(2)}) copy-start(f32[1,1,4096]{2,1,0:T(1,128)S(1)} %get-tuple-element.38) | copy-start | bytes 49156
  11.9 29.8 %copy-start.24 = (f32[1,1,4096]{2,1,0:T(1,128)}, f32[1,1,4096]{2,1,0:T(1,128)S(1)}, u32[]{:S(2)}) copy-start(f32[1,1,4096]{2,1,0:T(1,128)S(1)} %get-tuple-element.41) | copy-start | bytes 49156
  11.9 29.8 %copy-start.26 = (f32[1,1,4096]{2,1,0:T(1,128)}, f32[1,1,4096]{2,1,0:T(1,128)S(1)}, u32[]{:S(2)}) copy-start(f32[1,1,4096]{2,1,0:T(1,128)S(1)} %get-tuple-element.34) | copy-start | bytes 49156
  11.9 29.8 %copy-start.28 = (f32[1,1,4096]{2,1,0:T(1,128)}, f32[1,1,4096]{2,1,0:T(1,128)S(1)}, u32[]{:S(2)}) copy-start(f32[1,1,4096]{2,1,0:T(1,128)S(1)} %get-tuple-element.35) | copy-start | bytes 49156
  12.0 29.8 %copy-start.30 = (f32[1,1,4096]{2,1,0:T(1,128)}, f32[1,1,4096]{2,1,0:T(1,128)S(1)}, u32[]{:S(2)}) copy-start(f32[1,1,4096]{2,1,0:T(1,128)S(1)} %get-tuple-element.40) | copy-start | bytes 49156
  34.2 6.3 collective-permute-start
  46.5 16.1 %copy-start.32 = (f32[8192]{0:T(1024)S(1)}, f32[8192]{0:T(1024)}, u32[]{:S(2)}) copy-start(f32[8192]{0:T(1024)} %iota_convert_fusion) | copy-start | bytes 98308
  52.2 169.0 %all-to-all-start.2 = ((f32[1,4096,128]{2,0,1:T(1,128)}), f32[1,4096,128]{2,0,1:T(1,128)S(1)}, u32[]{:S(2)}, u32[]{:S(2)}) async-start(f32[1,4096,128]{2,0,1:T(1,128)} %copy.93), calls=%async_computation.2 | async-start | bytes 4194304 | tf_op jit(solution)/shard_map/all_to_all | solution.py:139
  200.5 9.5 %copy-start.4 = (f32[128,64,128]{2,0,1:T(8,128)}, f32[128,64,128]{2,0,1:T(8,128)S(1)}, u32[]{:S(2)}) copy-start(f32[128,64,128]{2,0,1:T(8,128)S(1)} %fusion.175) | copy-start | bytes 12582916
  221.2 40.8 %all-to-all-start = ((f32[1,4096,128]{2,0,1:T(1,128)}), f32[1,4096,128]{2,0,1:T(1,128)}, u32[]{:S(2)}, u32[]{:S(2)}) async-start(f32[1,4096,128]{2,0,1:T(1,128)} %copy.85), calls=%async_computation | async-start | bytes 4194304 | tf_op jit(solution)/shard_map/all_to_all | solution.py:138
  232.2 9.8 %copy-start.17 = (f32[64,128,128]{2,1,0:T(8,128)S(1)}, f32[64,128,128]{2,1,0:T(8,128)}, u32[]{:S(2)}) copy-start(f32[64,128,128]{2,1,0:T(8,128)} %fusion.29) | copy-start | bytes 12582916
  401.6 81.5 %all-to-all-start.3 = ((f32[64,1,8192]{2,1,0:T(1,128)}), f32[64,1,8192]{2,1,0:T(1,128)}, u32[]{:S(2)}, u32[]{:S(2)}) async-start(f32[64,1,8192]{2,1,0:T(1,128)} %reshape.405), calls=%async_computation.3 | async-start | bytes 4194304 | tf_op jit(solution)/shard_map/all_to_all | solution.py:145
  483.1 39.6 %all-to-all-start.1 = ((f32[64,1,8192]{2,1,0:T(1,128)}), f32[64,1,8192]{2,1,0:T(1,128)}, u32[]{:S(2)}, u32[]{:S(2)}) async-start(f32[64,1,8192]{2,1,0:T(1,128)} %reshape.403), calls=%async_computation.1 | async-start | bytes 4194304 | tf_op jit(solution)/shard_map/all_to_all | solution.py:144
  493.6 114.0 %reduce-scatter.2.cloned.1.call-start = ((), (), s32[]{:S(2)}) async-start(), calls=%async_computation.6 | async-start | bytes 12582912 | tf_op jit(solution)/shard_map/reduce_scatter | solution.py:174
  554.6 11.8 %copy-start.21 = (f32[1,1,4096]{2,1,0:T(1,128)S(1)}, f32[1,1,4096]{2,1,0:T(1,128)}, u32[]{:S(2)}) copy-start(f32[1,1,4096]{2,1,0:T(1,128)} %copy-done.20) | copy-start | bytes 49156
  554.6 11.8 %copy-start.23 = (f32[1,1,4096]{2,1,0:T(1,128)S(1)}, f32[1,1,4096]{2,1,0:T(1,128)}, u32[]{:S(2)}) copy-start(f32[1,1,4096]{2,1,0:T(1,128)} %copy-done.22) | copy-start | bytes 49156
  554.7 11.8 %copy-start.25 = (f32[1,1,4096]{2,1,0:T(1,128)S(1)}, f32[1,1,4096]{2,1,0:T(1,128)}, u32[]{:S(2)}) copy-start(f32[1,1,4096]{2,1,0:T(1,128)} %copy-done.24) | copy-start | bytes 49156
  566.5 9.9 %copy-start.14 = (f32[1,4096,128]{1,2,0:T(8,128)S(1)}, f32[1,4096,128]{1,2,0:T(8,128)}, u32[]{:S(2)}) copy-start(f32[1,4096,128]{1,2,0:T(8,128)} %get-tuple-element.15) | copy-start | bytes 6291460
  566.5 9.9 %copy-start.15 = (f32[1,4096,128]{1,2,0:T(8,128)S(1)}, f32[1,4096,128]{1,2,0:T(8,128)}, u32[]{:S(2)}) copy-start(f32[1,4096,128]{1,2,0:T(8,128)} %get-tuple-element.16) | copy-start | bytes 6291460
  566.5 9.9 %copy-start.16 = (f32[1,4096,128]{1,2,0:T(8,128)S(1)}, f32[1,4096,128]{1,2,0:T(8,128)}, u32[]{:S(2)}) copy-start(f32[1,4096,128]{1,2,0:T(8,128)} %get-tuple-element.17) | copy-start | bytes 6291460
  566.5 9.9 %copy-start.18 = (f32[1,4096,128]{1,2,0:T(8,128)S(1)}, f32[1,4096,128]{1,2,0:T(8,128)}, u32[]{:S(2)}) copy-start(f32[1,4096,128]{1,2,0:T(8,128)} %get-tuple-element.14) | copy-start | bytes 6291460
  566.5 9.9 %copy-start.27 = (f32[1,1,4096]{2,1,0:T(1,128)S(1)}, f32[1,1,4096]{2,1,0:T(1,128)}, u32[]{:S(2)}) copy-start(f32[1,1,4096]{2,1,0:T(1,128)} %copy-done.26) | copy-start | bytes 49156
  566.5 9.9 %copy-start.29 = (f32[1,1,4096]{2,1,0:T(1,128)S(1)}, f32[1,1,4096]{2,1,0:T(1,128)}, u32[]{:S(2)}) copy-start(f32[1,1,4096]{2,1,0:T(1,128)} %copy-done.28) | copy-start | bytes 49156
  566.6 9.9 %copy-start.31 = (f32[1,1,4096]{2,1,0:T(1,128)S(1)}, f32[1,1,4096]{2,1,0:T(1,128)}, u32[]{:S(2)}) copy-start(f32[1,1,4096]{2,1,0:T(1,128)} %copy-done.30) | copy-start | bytes 49156
  566.6 9.9 %copy-start.34 = (s32[1,128]{1,0:T(1,128)S(1)}, s32[1,128]{1,0:T(1,128)}, u32[]{:S(2)}) copy-start(s32[1,128]{1,0:T(1,128)} %param.8) | copy-start | bytes 1540
  570.1 6.3 collective-permute-start.1
  583.0 24.6 %copy-start.19 = (f32[1,4096,128]{1,2,0:T(8,128)S(1)}, f32[1,4096,128]{1,2,0:T(8,128)}, u32[]{:S(2)}) copy-start(f32[1,4096,128]{1,2,0:T(8,128)} %get-tuple-element.29) | copy-start | bytes 6291460
  583.0 170.5 %all-reduce.2.cloned.1.call-start = ((), (), s32[]{:S(2)}) async-start(), calls=%async_computation.7 | async-start | bytes 8388608 | tf_op jit(solution)/shard_map/psum | solution.py:175
  607.6 150.6 %copy-start.1 = (s32[4096,16]{0,1:T(8,128)S(1)}, s32[4096,16]{0,1:T(8,128)}, u32[]{:S(2)}) copy-start(s32[4096,16]{0,1:T(8,128)} %param.13) | copy-start | bytes 786436
  (12 other events, 72.6 us)
Sparse Core Ops, SparseCore 0:
  9.7 18.7 all-gather.1
  583.1 24.4 reduce-scatter.1
  613.4 140.0 all-reduce.1
where the time goes:
time: 772 us; the launch traced here: 765 us
  other arithmetic  249 us (32%)
  waiting for transfers between devices  191 us (25%)
  matrix products  170 us (22%)
  local copies, waits for them, and re-layouts  92 us (12%)
  starting transfers between devices  48.6 us (6%)
  between operations  14.7 us (2%)
    psum x1, waiting for transfers between devices, body(): embed_grad = lax.psum(half_grad, 'ctx')  144 us
    reduce_sum x1, other arithmetic, body(): jnp.sum(weight * jnp.exp(-decay_rate * positions.astype(jnp.float32)[None...  133 us
    unnamed x2, other arithmetic  76.8 us
    unnamed x79, local copies, waits for them, and re-layouts  34.9 us
    dot_general x3, matrix products, forward_dft(): jnp.einsum('bckt,tm->bckm', turned_imag, inner_sin, precision=HIGHEST)  30.9 us
    reduce_scatter x1, waiting for transfers between devices, body(): lax.psum_scatter(partial_grad, 'fsdp', scatter_dimension=1, tiled=True)  24.6 us
    dot_general x3, matrix products, forward_dft(): jnp.einsum('bckt,tm->bckm', turned_imag, inner_cos, precision=HIGHEST)  20.6 us
    all_to_all x3, local copies, waits for them, and re-layouts, body(): lax.all_to_all(conv_part, 'ctx', split_axis=2, concat_axis=1, tiled=True)  17.7 us
  transfers between devices with their start and end apart: 9, of which 4 were waited for; matrix products, arithmetic and copies ran while one was open for 39% of the time, Pallas kernels for 0%

commit v1 on v0

--- a/solution.py
+++ b/solution.py
@@ -172,7 +172,7 @@
     ).astype(jnp.float32)
     partial_grad = jnp.einsum("btv,bct->vc", one_hot, grad_signal, precision=HIGHEST)
     half_grad = lax.psum_scatter(partial_grad, "fsdp", scatter_dimension=1, tiled=True)
-    embed_grad = lax.psum(half_grad, "ctx")
+    embed_grad = jnp.sum(lax.all_gather(half_grad, "ctx"), axis=0)
     return (mixer_local, embed_grad)
 
 

time: 772 us -> 1700 us (2.20)
  waiting for transfers between devices: 191 us -> 1040 us
  other arithmetic: 249 us -> 331 us
    all_gather x0 -> x1, waiting for transfers between devices: none -> 991 us  [body(): embed_grad = jnp.sum(lax.all_gather(half_grad, 'ctx'), axis=0)]
    psum x1 -> x0, waiting for transfers between devices: 144 us -> none  [body(): embed_grad = lax.psum(half_grad, 'ctx')]
    reduce_sum x0 -> x1, other arithmetic: none -> 82.3 us  [body(): embed_grad = jnp.sum(lax.all_gather(half_grad, 'ctx'), axis=0)]
    unnamed x79 -> x78, local copies, waits for them, and re-layouts: 34.9 us -> 30.2 us
  transfers between devices with their start and end apart: 9 -> 9, of which waited for: 4 -> 4; matrix products, arithmetic and copies ran while one was open for 39% -> 17% of each run, Pallas kernels for 0% -> 0%
where the time goes in v1:
time: 1700 us; the launch traced here: 1690 us
  waiting for transfers between devices  1040 us (61%)
  other arithmetic  331 us (19%)
  matrix products  170 us (10%)
  local copies, waits for them, and re-layouts  87.4 us (5%)
  starting transfers between devices  48.6 us (3%)
    all_gather x1, waiting for transfers between devices, body(): embed_grad = jnp.sum(lax.all_gather(half_grad, 'ctx'), axis=0)  991 us
    reduce_sum x1, other arithmetic, body(): jnp.sum(weight * jnp.exp(-decay_rate * positions.astype(jnp.float32)[None...  133 us
    reduce_sum x1, other arithmetic, body(): embed_grad = jnp.sum(lax.all_gather(half_grad, 'ctx'), axis=0)  82.3 us
    unnamed x2, other arithmetic  76.8 us
  transfers between devices with their start and end apart: 9, of which 4 were waited for; matrix products, arithmetic and copies ran while one was open for 17% of the time, Pallas kernels for 0%

profile of v1, /device:TPU:0, one launch (start us, length us, event | category | flops | bytes accessed | tf_op | source)
XLA Modules:
  0.0 1689.4 jit_solution(7698383766879408301)
XLA Ops:
  12.1 16.4 all-gather.4.cloned.1.call-done
  52.2 10.4 all-to-all-start.2
  62.6 133.4 %fusion.5 = f32[64,8192]{1,0:T(8,128)S(1)} fusion(s32[64,16]{1,0:T(8,128)S(1)} %copy.84, f32[8192]{0:T(1024)S(1)} %copy-done.32, f32[64,16]{1,0:T(8,128)S(1)} %copy.83, f32[64,16]{1,0:T(8,128)S(1)} %copy.82), kind=kLoop, calls=%fused_computation.9 | loop fusion | flops 150470656 | bytes 2142208 | tf_op jit(solution)/shard_map/reduce_sum | solution.py:127
  204.2 5.8 fusion.27
  221.2 10.9 all-to-all-start
  232.2 8.8 fusion.58
  242.0 5.7 fusion.55
  247.7 7.0 fusion.81
  254.7 7.3 fusion.83
  262.1 6.3 fusion.85
  268.4 6.3 fusion.87
  293.1 6.0 fusion.64
  299.1 5.8 fusion.61
  304.9 5.8 fusion.70
  310.8 19.4 %multiply_add_fusion = (f32[64,128,128]{2,1,0:T(8,128)}, f32[64,128,128]{2,1,0:T(8,128)}, f32[64,128,128]{2,1,0:T(8,128)}, f32[64,128,128]{2,1,0:T(8,128)}) fusion(f32[64,128,128]{2,1,0:T(8,128)} %fusion.55, f32[64,128,128]{2,1,0:T(8,128)} %fusion.70, f32[64,128,128]{2,1,0:T(8,128)} %fusion.58, f32[64,128,128]{2,1,0:T(8,128)} %fusion.64, ...), kind=kOutput, calls=%fused_computation.63 | convolution fusion | flops 1629716480 | bytes 50462720 | tf_op jit(solution)/shard_map/bckt,tm->bckm/dot_general | solution.py:55
  330.1 6.5 fusion.147
  357.7 38.4 %reduce.2 = f32[8192,64]{1,0:T(8,128)} reduce(f32[8192,1,64]{2,1,0:T(1,128)} %bitcast.331, f32[]{:T(128)} %broadcast.309), dimensions={1}, to_apply=%bitcast.305.reduce_sub_computation | reduce | bytes 4194308
  401.6 10.7 all-to-all-start.3
  412.3 6.4 fusion.155
  439.2 38.4 %reduce = f32[8192,64]{1,0:T(8,128)} reduce(f32[8192,1,64]{2,1,0:T(1,128)} %bitcast.332, f32[]{:T(128)} %broadcast.309), dimensions={1}, to_apply=%bitcast.303.reduce_sub_computation | reduce | bytes 4194308
  483.1 10.5 all-to-all-start.1
  494.0 7.5 reduce.3
  501.6 6.6 reshape.407
  508.1 9.1 copy.96
  522.7 7.5 reduce.1
  530.2 6.8 reshape.405
  536.9 10.5 copy.88
  554.7 10.9 multiply_add_fusion.3
  576.6 6.5 fusion.75
  583.1 24.6 %reduce-scatter.2.cloned.1.call-done = f32[512,2048]{1,0:T(8,128)} async-done(((f32[512,4096]{1,0:T(8,128)}), f32[512,2048]{1,0:T(8,128)}) %reduce-scatter.2.cloned.1.call-update) | async-done | bytes 4194320 | tf_op jit(solution)/shard_map/reduce_scatter | solution.py:174
  609.5 990.8 %all-gather.6.cloned.1.call-done = f32[32768,2048]{1,0:T(8,128)} async-done(((f32[512,2048]{1,0:T(8,128)}), f32[32768,2048]{1,0:T(8,128)}) %all-gather.6.cloned.1.call-update) | async-done | bytes 268435456 | tf_op jit(solution)/shard_map/all_gather | solution.py:175
  1600.3 82.3 %reduce_sum.19 = f32[512,2048]{1,0:T(8,128)} reduce(f32[64,512,2048]{2,1,0:T(8,128)} %bitcast.68, f32[]{:T(128)} %constant.81.clone.1), dimensions={0}, to_apply=%region_2.3 | reduce | flops 66060288 | bytes 272629760 | tf_op jit(solution)/shard_map/reduce_sum | solution.py:175
  (136 shorter events, 145.3 us)
Async XLA Ops:
  7.2 31.2 %copy-start = (s32[4096,16]{0,1:T(8,128)S(1)}, s32[4096,16]{0,1:T(8,128)}, u32[]{:S(2)}) copy-start(s32[4096,16]{0,1:T(8,128)} %param.13) | copy-start | bytes 786436
  7.2 21.3 %all-gather.4.cloned.1.call-start = ((), (), s32[]{:S(2)}) async-start(), calls=%async_computation.5 | async-start | bytes 6291456 | tf_op jit(solution)/shard_map/all_gather | solution.py:100
  12.0 29.7 %copy-start.20 = (f32[1,1,4096]{2,1,0:T(1,128)}, f32[1,1,4096]{2,1,0:T(1,128)S(1)}, u32[]{:S(2)}) copy-start(f32[1,1,4096]{2,1,0:T(1,128)S(1)} %get-tuple-element.36) | copy-start | bytes 49156
  12.0 29.7 %copy-start.22 = (f32[1,1,4096]{2,1,0:T(1,128)}, f32[1,1,4096]{2,1,0:T(1,128)S(1)}, u32[]{:S(2)}) copy-start(f32[1,1,4096]{2,1,0:T(1,128)S(1)} %get-tuple-element.38) | copy-start | bytes 49156
  12.0 29.7 %copy-start.24 = (f32[1,1,4096]{2,1,0:T(1,128)}, f32[1,1,4096]{2,1,0:T(1,128)S(1)}, u32[]{:S(2)}) copy-start(f32[1,1,4096]{2,1,0:T(1,128)S(1)} %get-tuple-element.41) | copy-start | bytes 49156
  12.0 29.7 %copy-start.26 = (f32[1,1,4096]{2,1,0:T(1,128)}, f32[1,1,4096]{2,1,0:T(1,128)S(1)}, u32[]{:S(2)}) copy-start(f32[1,1,4096]{2,1,0:T(1,128)S(1)} %get-tuple-element.34) | copy-start | bytes 49156
  12.0 29.7 %copy-start.28 = (f32[1,1,4096]{2,1,0:T(1,128)}, f32[1,1,4096]{2,1,0:T(1,128)S(1)}, u32[]{:S(2)}) copy-start(f32[1,1,4096]{2,1,0:T(1,128)S(1)} %get-tuple-element.35) | copy-start | bytes 49156
  12.0 29.7 %copy-start.30 = (f32[1,1,4096]{2,1,0:T(1,128)}, f32[1,1,4096]{2,1,0:T(1,128)S(1)}, u32[]{:S(2)}) copy-start(f32[1,1,4096]{2,1,0:T(1,128)S(1)} %get-tuple-element.40) | copy-start | bytes 49156
  34.2 6.3 collective-permute-start
  46.5 16.1 copy-start.32
  52.2 169.0 %all-to-all-start.2 = ((f32[1,4096,128]{2,0,1:T(1,128)}), f32[1,4096,128]{2,0,1:T(1,128)S(1)}, u32[]{:S(2)}, u32[]{:S(2)}) async-start(f32[1,4096,128]{2,0,1:T(1,128)} %copy.93), calls=%async_computation.2 | async-start | bytes 4194304 | tf_op jit(solution)/shard_map/all_to_all | solution.py:139
  200.5 9.5 copy-start.4
  221.2 40.8 %all-to-all-start = ((f32[1,4096,128]{2,0,1:T(1,128)}), f32[1,4096,128]{2,0,1:T(1,128)}, u32[]{:S(2)}, u32[]{:S(2)}) async-start(f32[1,4096,128]{2,0,1:T(1,128)} %copy.85), calls=%async_computation | async-start | bytes 4194304 | tf_op jit(solution)/shard_map/all_to_all | solution.py:138
  232.2 9.8 copy-start.17
  401.6 81.5 %all-to-all-start.3 = ((f32[64,1,8192]{2,1,0:T(1,128)}), f32[64,1,8192]{2,1,0:T(1,128)}, u32[]{:S(2)}, u32[]{:S(2)}) async-start(f32[64,1,8192]{2,1,0:T(1,128)} %reshape.406), calls=%async_computation.3 | async-start | bytes 4194304 | tf_op jit(solution)/shard_map/all_to_all | solution.py:145
  483.1 39.6 %all-to-all-start.1 = ((f32[64,1,8192]{2,1,0:T(1,128)}), f32[64,1,8192]{2,1,0:T(1,128)}, u32[]{:S(2)}, u32[]{:S(2)}) async-start(f32[64,1,8192]{2,1,0:T(1,128)} %reshape.404), calls=%async_computation.1 | async-start | bytes 4194304 | tf_op jit(solution)/shard_map/all_to_all | solution.py:144
  493.6 114.1 %reduce-scatter.2.cloned.1.call-start = ((), (), s32[]{:S(2)}) async-start(), calls=%async_computation.6 | async-start | bytes 12582912 | tf_op jit(solution)/shard_map/reduce_scatter | solution.py:174
  554.6 11.9 copy-start.21
  554.6 11.9 copy-start.23
  554.7 11.9 copy-start.25
  566.6 9.9 copy-start.14
  566.6 9.9 copy-start.15
  566.6 9.9 copy-start.16
  566.6 9.9 copy-start.18
  566.6 9.9 copy-start.27
  566.6 9.9 copy-start.29
  566.6 9.9 copy-start.31
  566.6 9.9 copy-start.34
  570.2 6.3 collective-permute-start.1
  583.1 24.6 %copy-start.19 = (f32[1,4096,128]{1,2,0:T(8,128)S(1)}, f32[1,4096,128]{1,2,0:T(8,128)}, u32[]{:S(2)}) copy-start(f32[1,4096,128]{1,2,0:T(8,128)} %get-tuple-element.29) | copy-start | bytes 6291460
  583.1 1017.3 %all-gather.6.cloned.1.call-start = ((), (), s32[]{:S(2)}) async-start(), calls=%async_computation.7 | async-start | bytes 272629760 | tf_op jit(solution)/shard_map/all_gather | solution.py:175
  1600.3 82.3 %copy-start.1 = (s32[4096,16]{0,1:T(8,128)S(1)}, s32[4096,16]{0,1:T(8,128)}, u32[]{:S(2)}) copy-start(s32[4096,16]{0,1:T(8,128)} %param.13) | copy-start | bytes 786436
  (12 other events, 72.6 us)
Sparse Core Ops, SparseCore 0:
  9.7 18.7 all-gather.3
  583.2 24.4 reduce-scatter.1
  611.0 989.3 all-gather.5
